TPU v7x, 32 devices: a whole 2x2x4 slice. The times are simulated.
32 devices in a mesh: ctx: 4 (over z), tp: 2 (over x), dp: 4 (over y, core).
Axes of the slice: x: 2, y: 2, z: 4, core: 2. Of those that a mesh axis runs over, the one named last changes fastest.
Arguments:
- queries: bfloat16 [4, 1024, 8192], P('dp', 'ctx', 'tp'), may hold values from -80 to 80
- prompt_keys: bfloat16 [4, 1024, 1024], P('dp', 'ctx', 'tp'), may hold values from -4 to 4
- prompt_values: bfloat16 [4, 1024, 1024], P('dp', 'ctx', 'tp'), may hold values from -6 to 6
- resp_keys: bfloat16 [4, 1024, 1024], P('dp', 'ctx', 'tp'), may hold values from -4 to 4
- resp_values: bfloat16 [4, 1024, 1024], P('dp', 'ctx', 'tp'), may hold values from -6 to 6
- pattern: int32 [4, 2, 8], P('dp'), may hold values from 0 to 1, as said below
- lengths: int32 [4, 2], P('dp'), may hold values from 257 to 512, as said below
- out_weight: bfloat16 [8192, 4096], P(('tp', 'dp'), 'ctx'), may hold values from -0.0625 to 0.0625
Outputs:
- attended: bfloat16 [4, 1024, 4096], P('dp', 'ctx', 'tp')
Inputs may be any that keep to these rules, and one draw needn't show every extreme that they name: pattern[g, r, 0] is 1 for every response; each response reads 4 or more blocks; in each group some response reads all 8 blocks. `lengths`: in each group some response has length 512.
All inputs are finite; a program needn't handle non-finite values.
Results may differ from a plain program's by a relative error of at most 0.013.
Values may be sent and summed in bfloat16 or wider, within the bound.
A program may use at most 192 MiB of HBM per device.

v0:
```python
import jax
import jax.numpy as jnp
from jax import lax
from jax.sharding import PartitionSpec as P

HD = 128
BLK = 128
RLEN = 512


def shifted(x, axis, by):
    devices = lax.axis_size(axis)
    pairs = [(i, i + by) for i in range(devices) if 0 <= i + by < devices]
    return lax.ppermute(x, axis, pairs)


def local(
    queries, prompt_keys, prompt_values, resp_keys, resp_values, pattern, lengths, out_weight
):
    tok = queries.shape[1]
    kv_here = prompt_keys.shape[2] // HD
    q_here = queries.shape[2] // HD
    group = q_here // kv_here
    scale = HD ** (-0.5)
    halves = RLEN // tok
    responses = lax.axis_size("ctx") // halves
    place = lax.axis_index("ctx")
    resp_id = place % responses
    half = place // responses
    positions = half * tok + jnp.arange(tok, dtype=jnp.int32)
    chosen = jnp.arange(pattern.shape[1], dtype=jnp.int32) == resp_id
    block_row = jnp.sum(jnp.where(chosen[:, None], pattern[0], 0), axis=0)
    live_len = jnp.sum(jnp.where(chosen, lengths[0], 0))
    query_heads = queries[0].reshape(tok, kv_here, group, HD)
    earlier = shifted((resp_keys, resp_values), "ctx", responses)
    own_keys = jnp.concatenate([earlier[0][0], resp_keys[0]], axis=0).reshape(2 * tok, kv_here, HD)
    own_vals = jnp.concatenate([earlier[1][0], resp_values[0]], axis=0).reshape(
        2 * tok, kv_here, HD
    )
    key_pos = (half - 1) * tok + jnp.arange(2 * tok, dtype=jnp.int32)
    allowed = (key_pos[None, :] >= 0) & (key_pos[None, :] <= positions[:, None])
    scores = (
        jnp.einsum("ikgd,jkd->kgij", query_heads, own_keys, preferred_element_type=jnp.float32)
        * scale
    )
    running = jnp.max(jnp.where(allowed, scores, -jnp.inf), axis=-1)
    probs = jnp.where(allowed, jnp.exp(scores - running[..., None]), 0.0)
    total = jnp.sum(probs, axis=-1)
    accum = jnp.einsum(
        "kgij,jkd->kgid", probs.astype(jnp.bfloat16), own_vals, preferred_element_type=jnp.float32
    )
    pieces = (
        lax.all_gather(prompt_keys, "ctx", axis=1, tiled=True),
        lax.all_gather(prompt_values, "ctx", axis=1, tiled=True),
    )
    count = pieces[0].shape[1]
    block_ids = jnp.arange(count, dtype=jnp.int32) // BLK
    onehot = block_ids[:, None] == jnp.arange(block_row.shape[0], dtype=jnp.int32)[None, :]
    readable = jnp.sum(jnp.where(onehot, block_row[None, :], 0), axis=1) > 0
    piece_keys = pieces[0][0].reshape(-1, kv_here, HD)
    piece_vals = pieces[1][0].reshape(-1, kv_here, HD)
    block_scores = (
        jnp.einsum("ikgd,jkd->kgij", query_heads, piece_keys, preferred_element_type=jnp.float32)
        * scale
    )
    mask = readable[None, None, None, :]
    new_max = jnp.maximum(running, jnp.max(jnp.where(mask, block_scores, -jnp.inf), axis=-1))
    weights = jnp.where(mask, jnp.exp(block_scores - new_max[..., None]), 0.0)
    factor = jnp.exp(running - new_max)
    new_total = total * factor + jnp.sum(weights, axis=-1)
    new_acc = accum * factor[..., None] + jnp.einsum(
        "kgij,jkd->kgid",
        weights.astype(jnp.bfloat16),
        piece_vals,
        preferred_element_type=jnp.float32,
    )
    context = new_acc / new_total[..., None]
    context = jnp.transpose(context, (2, 0, 1, 3)).reshape(tok, q_here * HD)
    context = jnp.where((positions < live_len)[:, None], context, 0.0).astype(jnp.bfloat16)
    head_rows = lax.all_gather(out_weight, "dp", axis=0, tiled=True)
    partial_out = jnp.dot(
        context,
        lax.all_gather(head_rows, "ctx", axis=1, tiled=True),
        preferred_element_type=jnp.float32,
    )
    summed = lax.psum_scatter(
        partial_out.astype(jnp.bfloat16), "tp", scatter_dimension=1, tiled=True
    )
    return summed[None]


def solution(mesh):
    placed = (
        P("dp", "ctx", "tp"),
        P("dp", "ctx", "tp"),
        P("dp", "ctx", "tp"),
        P("dp", "ctx", "tp"),
        P("dp", "ctx", "tp"),
        P("dp", None, None),
        P("dp", None),
        P(("tp", "dp"), "ctx"),
    )
    return jax.shard_map(
        local, mesh=mesh, in_specs=placed, out_specs=P("dp", "ctx", "tp"), check_vma=False
    )
```

profile of v0, /device:TPU:17, one launch (start us, length us, event | category | flops | bytes accessed | tf_op | source)
XLA Modules:
  0.0 757.0 jit_solution(10825526492452625463)
XLA Ops:
  6.5 0.7 all-gather.9.cloned.1.call-update
  7.3 1.8 copy.37
  9.2 0.7 all-gather.7.cloned.1.call-update
  9.9 58.8 %all-gather.9.cloned.1.call-done = bf16[4096,1024]{1,0:T(8,128)(2,1)} async-done(((bf16[1024,1024]{1,0:T(8,128)(2,1)}), bf16[4096,1024]{1,0:T(8,128)(2,1)}) %all-gather.9.cloned.1.call-update) | async-done | bytes 8388624 | tf_op jit(solution)/shard_map/all_gather | solution.py:80
  68.7 1.1 copy.29
  69.8 1.3 collective-permute-start
  71.1 1.3 collective-permute-start.1
  72.5 0.6 broadcast_compare_fusion.1
  73.1 1.3 fusion.33
  74.4 0.8 fusion.32
  75.2 0.6 broadcast_compare_fusion.2
  75.9 1.1 copy.35
  77.0 2.1 copy.50
  79.1 0.2 copy.32
  79.3 0.9 compare_and_fusion
  80.2 1.4 collective-permute-done
  81.5 0.2 copy.31
  81.7 11.1 %collective-permute-done.1 = bf16[1,256,512]{2,1,0:T(8,128)(2,1)S(1)} collective-permute-done((bf16[1,256,512]{2,1,0:T(8,128)(2,1)}, bf16[1,256,512]{2,1,0:T(8,128)(2,1)S(1)}, u32[]{:S(2)}, u32[]{:S(2)}) %collective-permute-start.1) | collective-permute-done | bytes 262176 | tf_op jit(solution)/shard_map/ppermute | solution.py:14
  92.8 0.1 copy.34
  92.9 7.3 fusion.5
  100.2 9.2 %fusion.11 = f32[4,8,256]{2,1,0:T(8,128)S(1)} fusion(f32[4,512,256,8]{2,1,3,0:T(8,128)} %get-tuple-element.8, f32[4,8,256]{2,1,0:T(8,128)S(1)} %get-tuple-element.7, pred[256,512]{0,1:T(8,128)(4,1)S(1)} %compare_and_fusion), kind=kLoop, calls=%fused_computation.14 | loop fusion | flops 16769024 | bytes 16973824 | tf_op jit(solution)/shard_map/reduce_sum | solution.py:48
  109.4 2.1 all-gather.5.cloned.1.call-done
  111.5 16.0 %fusion = (f32[4,8,256]{2,1,0:T(8,128)S(1)}, f32[4,1024,256,8]{2,1,3,0:T(8,128)}) fusion(pred[1024]{0:T(1024)(128)(4,1)S(1)} %broadcast_compare_fusion, bf16[1024,4,128,1]{0,2,3,1:T(8,128)(2,1)} %bitcast.100, bf16[256,4,8,128]{3,2,1,0:T(8,128)(2,1)S(1)} %bitcast.98), kind=kOutput, calls=%fused_computation.2 | convolution fusion | flops 2172641280 | bytes 36733952 | tf_op jit(solution)/shard_map/ikgd,jkd->kgij/dot_general | solution.py:63
  127.5 12.9 %all-gather.7.cloned.1.call-done = bf16[1,1024,512]{2,1,0:T(8,128)(2,1)} async-done(((bf16[1,256,512]{2,1,0:T(8,128)(2,1)}), bf16[1,1024,512]{2,1,0:T(8,128)(2,1)}) %all-gather.7.cloned.1.call-update) | async-done | bytes 1048592 | tf_op jit(solution)/shard_map/all_gather | solution.py:54
  140.4 1.5 copy.40
  141.9 17.4 %fusion.3 = f32[4,8,256]{2,1,0:T(8,128)S(1)} fusion(f32[4,1024,256,8]{2,1,3,0:T(8,128)} %get-tuple-element.10, f32[4,8,256]{2,1,0:T(8,128)S(1)} %max.18, pred[1024]{0:T(1024)(128)(4,1)S(1)} %broadcast_compare_fusion), kind=kLoop, calls=%fused_computation.5 | loop fusion | flops 33546240 | bytes 33620992 | tf_op jit(solution)/shard_map/reduce_sum | solution.py:70
  159.4 17.1 %fusion.8 = f32[4,8,256,128]{2,3,1,0:T(8,128)S(1)} fusion(bf16[1024,4,128,1]{0,2,3,1:T(8,128)(2,1)S(1)} %bitcast.101, f32[4,1024,256,8]{2,1,3,0:T(8,128)} %get-tuple-element.10, f32[4,8,256]{2,1,0:T(8,128)S(1)} %max.18, pred[1024]{0:T(1024)(128)(4,1)S(1)} %broadcast_compare_fusion), kind=kOutput, calls=%fused_computation.12 | convolution fusion | flops 2181038080 | bytes 38831104 | tf_op jit(solution)/shard_map/kgij,jkd->kgid/dot_general | solution.py:71
  176.5 7.8 %fusion.17 = bf16[256,4,8,128]{0,3,2,1:T(8,128)(2,1)S(1)} fusion(f32[4,8,256,128]{2,3,1,0:T(8,128)S(1)} %fusion.8, f32[4,512,256,8]{2,1,3,0:T(8,128)} %get-tuple-element.8, f32[4,8,256]{2,1,0:T(8,128)S(1)} %get-tuple-element.7, pred[256,512]{0,1:T(8,128)(4,1)S(1)} %compare_and_fusion, f32[256,4,8]{0,2,1:T(8,128)S(1)} %get-tuple-element.5, ...), kind=kOutput, calls=%fused_computation.22 | convolution fusion | flops 1095761920 | bytes 23822336 | tf_op jit(solution)/shard_map/kgij,jkd->kgid/dot_general | solution.py:49
  184.3 0.5 fusion.16
  184.8 516.9 %all-gather.11.cloned.1.call-done = bf16[4096,4096]{1,0:T(8,128)(2,1)} async-done(((bf16[4096,1024]{1,0:T(8,128)(2,1)}), bf16[4096,4096]{1,0:T(8,128)(2,1)}) %all-gather.11.cloned.1.call-update) | async-done | bytes 33554448 | tf_op jit(solution)/shard_map/all_gather | solution.py:83
  701.7 16.7 %convolution_convert_fusion = bf16[256,4096]{1,0:T(8,128)(2,1)} fusion(bf16[256,4096]{0,1:T(8,128)(2,1)S(1)} %fusion.16, bf16[4096,4096]{1,0:T(8,128)(2,1)} %all-gather.11.cloned.1.call-done), kind=kOutput, calls=%fused_computation.18 | convolution fusion | flops 8590983168 | bytes 37748736 | tf_op jit(solution)/shard_map/dot_general | solution.py:81
  718.4 32.0 %reduce-scatter.2.cloned.1.call-done = bf16[256,2048]{1,0:T(8,128)(2,1)} async-done(((bf16[256,4096]{1,0:T(8,128)(2,1)}), bf16[256,2048]{1,0:T(8,128)(2,1)}) %reduce-scatter.2.cloned.1.call-update) | async-done | bytes 1048592 | tf_op jit(solution)/shard_map/reduce_scatter | solution.py:86
  (16 shorter events, 0.3 us)
Async XLA Ops:
  6.5 62.1 %all-gather.9.cloned.1.call-start = ((), (), s32[]{:S(2)}) async-start(), calls=%async_computation.3 | async-start | bytes 10485760 | tf_op jit(solution)/shard_map/all_gather | solution.py:80
  7.3 104.2 %all-gather.5.cloned.1.call-start = ((), (), s32[]{:S(2)}) async-start(), calls=%async_computation.1 | async-start | bytes 1310720 | tf_op jit(solution)/shard_map/all_gather | solution.py:53
  9.1 131.3 %all-gather.7.cloned.1.call-start = ((), (), s32[]{:S(2)}) async-start(), calls=%async_computation.2 | async-start | bytes 1310720 | tf_op jit(solution)/shard_map/all_gather | solution.py:54
  9.9 691.9 %all-gather.11.cloned.1.call-start = ((), (), s32[]{:S(2)}) async-start(), calls=%async_computation.4 | async-start | bytes 41943040 | tf_op jit(solution)/shard_map/all_gather | solution.py:83
  68.7 681.8 %reduce-scatter.2.cloned.1.call-start = ((), (), s32[]{:S(2)}) async-start(), calls=%async_computation.5 | async-start | bytes 3145728 | tf_op jit(solution)/shard_map/reduce_scatter | solution.py:86
  69.8 11.7 %collective-permute-start = (bf16[1,256,512]{1,2,0:T(8,128)(2,1)S(1)}, bf16[1,256,512]{1,2,0:T(8,128)(2,1)S(1)}, u32[]{:S(2)}, u32[]{:S(2)}) collective-permute-start(bf16[1,256,512]{1,2,0:T(8,128)(2,1)S(1)} %copy.29), channel_id=1, source_target_pairs={{0,16},{8,24},{1,17},{9,25},{2,18},{10,26},{3,19},{11,27},{4,20},{... | collective-permute-start | bytes 786440 | tf_op jit(solution)/shard_map/ppermute | solution.py:14
  71.1 21.6 %collective-permute-start.1 = (bf16[1,256,512]{2,1,0:T(8,128)(2,1)}, bf16[1,256,512]{2,1,0:T(8,128)(2,1)S(1)}, u32[]{:S(2)}, u32[]{:S(2)}) collective-permute-start(bf16[1,256,512]{2,1,0:T(8,128)(2,1)} %param.12), channel_id=1, source_target_pairs={{0,16},{8,24},{1,17},{9,25},{2,18},{10,26},{3,19},{11,27},{4,20},{... | collective-permute-start | bytes 786440 | tf_op jit(solution)/shard_map/ppermute | solution.py:14
Sparse Core Ops, SparseCore 0:
  8.9 59.7 all-gather.8
  70.2 41.1 all-gather.4
  113.0 27.3 all-gather.6
  141.8 559.8 all-gather.10
  718.6 31.8 reduce-scatter.1
where the time goes:
time: 759 us; the launch traced here: 757 us
  waiting for transfers between devices  637 us (84%)
  matrix products  64.9 us (9%)
  other arithmetic  31.4 us (4%)
  between operations  13.3 us (2%)
  local copies, waits for them, and re-layouts  8.06 us (1%)
    all_gather x1, waiting for transfers between devices, local(): lax.all_gather(head_rows, 'ctx', axis=1, tiled=True)  517 us
    all_gather x1, waiting for transfers between devices, local(): head_rows = lax.all_gather(out_weight, 'dp', axis=0, tiled=True)  58.8 us
    reduce_scatter x1, waiting for transfers between devices, local(): lax.psum_scatter(partial_out.astype(jnp.bfloat16), 'tp', scatter_dimensio...  32 us
    reduce_sum x1, other arithmetic, local(): new_total = total * factor + jnp.sum(weights, axis=-1)  17.4 us
    dot_general x1, matrix products, local(): jnp.einsum('kgij,jkd->kgid', weights.astype(jnp.bfloat16), piece_vals, pr...  17.1 us
    dot_general x1, matrix products, local(): jnp.dot(context, lax.all_gather(head_rows, 'ctx', axis=1, tiled=True), pr...  16.7 us
    dot_general x1, matrix products, local(): jnp.einsum('ikgd,jkd->kgij', query_heads, piece_keys, preferred_element_t...  16 us
  transfers between devices with their start and end apart: 7, of which 7 were waited for; matrix products, arithmetic and copies ran while one was open for 12% of the time, Pallas kernels for 0%

commit v1 on v0

--- a/solution.py
+++ b/solution.py
@@ -1,6 +1,8 @@
 import jax
 import jax.numpy as jnp
 from jax import lax
+from jax.experimental import pallas as pl
+from jax.experimental.pallas import tpu as pltpu
 from jax.sharding import PartitionSpec as P
 
 HD = 128
@@ -89,6 +91,354 @@
     return summed[None]
 
 
+MESH = pl.DeviceIdType.MESH
+CHUNKS = 4
+
+
+def kernel(
+    q_ref, pk_ref, pv_ref, rk_ref, rv_ref, bias_ref, live_ref, w_ref, o_ref,
+    kbuf, vbuf, ctx, wbuf, part, rbuf,
+    kv_send, kv_recv, rs_send, rs_recv, own_sem,
+    w_recv, w_send, fz_send, fy_send, c_send, c_recv, p_send, p_recv,
+):
+    z = lax.axis_index("ctx")
+    t = lax.axis_index("tp")
+    d = lax.axis_index("dp")
+    y, k = d // 2, d % 2
+    kz = z % 2
+    tok = q_ref.shape[0]
+    rows = w_ref.shape[0] // CHUNKS
+    wide = w_ref.shape[1]
+    pair_out = z // 2
+
+    def dev(zz, tt, yy, kk):
+        return {"ctx": zz, "tp": tt, "dp": yy * 2 + kk}
+
+    barrier = pltpu.get_barrier_semaphore()
+    greeted = [dev((z + i) % 4, t, y, k) for i in (1, 2, 3)]
+    greeted += [dev((z + i) % 4, t, y, 1 - k) for i in range(4)]
+    greeted += [dev(z, t, 1 - y, kk) for kk in range(2)]
+    greeted += [dev(z, 1 - t, y, kk) for kk in range(2)]
+    for other in greeted:
+        pl.semaphore_signal(barrier, inc=1, device_id=other, device_id_type=MESH)
+    pl.semaphore_wait(barrier, len(greeted))
+
+    def remote(src, dst, send, recv, where):
+        return pltpu.make_async_remote_copy(
+            src_ref=src, dst_ref=dst, send_sem=send, recv_sem=recv,
+            device_id=where, device_id_type=MESH,
+        )
+
+    def arrived(ref, sem):
+        pltpu.make_async_copy(ref, ref, sem).wait()
+
+    def prompt_rows(buf, zz):
+        return buf.at[pl.ds(pl.multiple_of(zz * tok, tok), tok), :]
+
+    pre = 4 * tok
+    kv = ((pk_ref, kbuf), (pv_ref, vbuf))
+    rkv = ((rk_ref, kbuf), (rv_ref, vbuf))
+    kv_copies = []
+    for step in (1, 3, 2):
+        for i, (src, buf) in enumerate(kv):
+            kv_copies.append(
+                remote(src, prompt_rows(buf, z), kv_send.at[i, step], kv_recv.at[i, step],
+                       dev((z + step) % 4, t, y, k))
+            )
+    for i, (src, buf) in enumerate(rkv):
+        kv_copies.append(
+            remote(src, buf.at[pl.ds(pre, tok), :], rs_send.at[i], rs_recv.at[i],
+                   dev((z + 2) % 4, t, y, k))
+        )
+    for copy in kv_copies:
+        copy.start()
+    own = []
+    for i, (src, buf) in enumerate(kv):
+        own.append(pltpu.make_async_copy(src, prompt_rows(buf, z), own_sem.at[i]))
+    for i, (src, buf) in enumerate(rkv):
+        own.append(
+            pltpu.make_async_copy(src, buf.at[pl.ds(pre + tok, tok), :], own_sem.at[2 + i])
+        )
+    for copy in own:
+        copy.start()
+
+    def w_slot(cc, dd, j):
+        return wbuf.at[cc, dd, pl.ds(pl.multiple_of(j * rows, rows), rows), :]
+
+    def own_rows(j):
+        return w_ref.at[pl.ds(pl.multiple_of(j * rows, rows), rows), :]
+
+    def own_send(target, j, where):
+        return remote(own_rows(j), w_slot(pair_out, d, j), w_send.at[target, j],
+                      w_recv.at[pair_out, d, j], where)
+
+    targets = (
+        (z < 3, dev(jnp.minimum(z + 1, 3), t, y, kz)),
+        (z > 0, dev(jnp.maximum(z - 1, 0), t, y, kz)),
+        (z >= 0, dev(z, t, 1 - y, kz)),
+        (k != kz, dev(z, t, y, 1 - k)),
+    )
+
+    def each_own(act):
+        @pl.loop(0, CHUNKS)
+        def _(j):
+            for n, (cond, where) in enumerate(targets):
+                @pl.when(cond)
+                def _(n=n, where=where):
+                    act(own_send(n, j, where))
+
+    each_own(lambda copy: copy.start())
+
+    @pl.when(k == kz)
+    def _():
+        @pl.loop(0, CHUNKS)
+        def _(j):
+            pltpu.make_async_copy(
+                own_rows(j), w_slot(pair_out, d, j), w_recv.at[pair_out, d, j]
+            ).start()
+
+    two = k != kz
+    middle = (z == 1) | (z == 2)
+    near_hi = z >= 2
+    cc_a = jnp.where(two, jnp.where(near_hi, 1, 0), 1 - pair_out)
+    cc_b = 1 - cc_a
+
+    def forwards(cc, n):
+        c = k + 2 * cc
+        dd = y * 2 + n // CHUNKS
+        j = n % CHUNKS
+        ref, rec = w_slot(cc, dd, j), w_recv.at[cc, dd, j]
+        up = (c < z) & (z < 3)
+        down = (c > z) & (z > 0)
+        zz = jnp.where(up, jnp.minimum(z + 1, 3), jnp.maximum(z - 1, 0))
+        along = remote(ref, ref, fz_send.at[cc, n], rec, dev(zz, t, y, k))
+        across = remote(ref, ref, fy_send.at[cc, n], rec, dev(z, t, 1 - y, k))
+        return ref, rec, up | down, along, across
+
+    def relay(cc, n):
+        ref, rec, onward, along, across = forwards(cc, n)
+        arrived(ref, rec)
+
+        @pl.when(onward)
+        def _():
+            along.start()
+
+        across.start()
+
+    for copy in own:
+        copy.wait()
+    for step in (1, 3, 2):
+        for i, (_, buf) in enumerate(kv):
+            arrived(prompt_rows(buf, (z + 4 - step) % 4), kv_recv.at[i, step])
+    for i, (_, buf) in enumerate(rkv):
+        arrived(buf.at[pl.ds(pre, tok), :], rs_recv.at[i])
+
+    scale = HD ** (-0.5)
+    heads = q_ref.shape[1] // HD
+    kv_here = rk_ref.shape[1] // HD
+    group = heads // kv_here
+    per = 2
+    mine = pl.ds(pl.multiple_of(k * tok, tok), tok)
+
+    def head(kk, g):
+        col = pl.multiple_of((kk * group + g) * HD, HD)
+        kcol = pl.multiple_of(kk * HD, HD)
+        gcol = pl.multiple_of(g * HD, HD)
+        s = lax.dot_general(
+            q_ref[:, pl.ds(col, HD)], kbuf[:, pl.ds(kcol, HD)], (((1,), (1,)), ((), ())),
+            preferred_element_type=jnp.float32,
+        )
+        s = s * scale + bias_ref[...]
+        p = jnp.exp(s - jnp.max(s, axis=-1, keepdims=True))
+        total = jnp.sum(p, axis=-1, keepdims=True)
+        o = jnp.dot(p.astype(jnp.bfloat16), vbuf[:, pl.ds(kcol, HD)],
+                    preferred_element_type=jnp.float32)
+        o = jnp.where(live_ref[...] > 0, o / total, 0.0)
+        ctx[kk, mine, pl.ds(gcol, HD)] = o.astype(jnp.bfloat16)
+
+    def ctx_send(kk):
+        ref = ctx.at[kk, mine, :]
+        return remote(ref, ref, c_send.at[kk], c_recv.at[kk], dev(z, t, y, 1 - k))
+
+    steps = heads // per
+    per_kv = group // per
+    slots = 2 * CHUNKS
+
+    @pl.loop(0, steps)
+    def _(it):
+        kk = it // per_kv
+        for u in range(per):
+            head(kk, (it % per_kv) * per + u)
+
+        @pl.when(it % per_kv == per_kv - 1)
+        def _():
+            ctx_send(kk).start()
+
+        @pl.when(two & (it < slots))
+        def _():
+            relay(cc_a, it)
+
+            @pl.when(middle)
+            def _():
+                relay(cc_b, it)
+
+        @pl.when(jnp.logical_not(two) & (it >= steps - slots))
+        def _():
+            relay(cc_a, it - (steps - slots))
+
+    theirs = pl.ds(pl.multiple_of((1 - k) * tok, tok), tok)
+
+    @pl.loop(0, kv_here)
+    def _(kk):
+        arrived(ctx.at[kk, theirs, :], c_recv.at[kk])
+
+    tile = 256
+
+    def out_send(cc, kk):
+        return remote(
+            part.at[cc, pl.ds(kk * tok, tok), :], rbuf.at[t, k], p_send.at[cc, kk],
+            p_recv.at[t, k], dev(z, cc, y, kk),
+        )
+
+    def out_sends(cc, act):
+        for kk in range(2):
+            @pl.when((cc != t) | (k != kk))
+            def _():
+                act(out_send(cc, kk))
+
+    def project(cc):
+        @pl.loop(0, slots)
+        def _(n):
+            dd = (1 - y) * 2 + n // CHUNKS
+            arrived(w_slot(cc, dd, n % CHUNKS), w_recv.at[cc, dd, n % CHUNKS])
+
+        @pl.when(k + 2 * cc == z)
+        def _():
+            @pl.loop(0, slots)
+            def _(n):
+                dd = y * 2 + n // CHUNKS
+                arrived(w_slot(cc, dd, n % CHUNKS), w_recv.at[cc, dd, n % CHUNKS])
+
+        @pl.loop(0, wide // tile)
+        def _(n):
+            cols = pl.ds(pl.multiple_of(n * tile, tile), tile)
+            acc = jnp.dot(ctx[0], wbuf[cc, 0, :, cols], preferred_element_type=jnp.float32)
+            for dd in range(1, kv_here):
+                acc += jnp.dot(
+                    ctx[dd], wbuf[cc, dd, :, cols], preferred_element_type=jnp.float32
+                )
+            part[cc, :, cols] = acc.astype(jnp.bfloat16)
+
+        @pl.when(cc == t)
+        def _():
+            rbuf[t, k] = part[cc, mine, :]
+
+        out_sends(cc, lambda copy: copy.start())
+
+    first = jnp.where(two, cc_a, cc_b)
+    second = 1 - first
+    project(first)
+
+    @pl.when(two & jnp.logical_not(middle))
+    def _():
+        @pl.loop(0, slots)
+        def _(n):
+            relay(cc_b, n)
+
+    project(second)
+
+    for copy in kv_copies:
+        copy.wait_send()
+    each_own(lambda copy: copy.wait_send())
+
+    def drain(cc):
+        @pl.loop(0, slots)
+        def _(n):
+            _, _, onward, along, across = forwards(cc, n)
+
+            @pl.when(onward)
+            def _():
+                along.wait_send()
+
+            across.wait_send()
+
+    drain(cc_a)
+
+    @pl.when(two)
+    def _():
+        drain(cc_b)
+
+    @pl.loop(0, kv_here)
+    def _(kk):
+        ctx_send(kk).wait_send()
+
+    for src in range(2):
+        for half in range(2):
+            @pl.when((t != src) | (k != half))
+            def _(src=src, half=half):
+                arrived(rbuf.at[src, half], p_recv.at[src, half])
+    for half in range(2):
+        both = rbuf[0, half].astype(jnp.float32) + rbuf[1, half].astype(jnp.float32)
+        o_ref[:, half * wide:(half + 1) * wide] = both.astype(jnp.bfloat16)
+    for cc in range(2):
+        out_sends(cc, lambda copy: copy.wait_send())
+
+
+def fused(
+    queries, prompt_keys, prompt_values, resp_keys, resp_values, pattern, lengths, out_weight
+):
+    tok = queries.shape[1]
+    halves = RLEN // tok
+    responses = lax.axis_size("ctx") // halves
+    place = lax.axis_index("ctx")
+    resp_id = place % responses
+    half = place // responses
+    chosen = jnp.arange(pattern.shape[1], dtype=jnp.int32) == resp_id
+    block_row = jnp.sum(jnp.where(chosen[:, None], pattern[0], 0), axis=0)
+    live_len = jnp.sum(jnp.where(chosen, lengths[0], 0))
+    slot = jnp.arange(tok, dtype=jnp.int32)
+    readable = jnp.repeat(block_row, BLK) > 0
+    earlier = jnp.broadcast_to(half > 0, (tok,))
+    keys_ok = jnp.concatenate([readable, earlier, jnp.ones((tok,), jnp.bool_)])
+    later = jnp.arange(keys_ok.shape[0], dtype=jnp.int32) - (keys_ok.shape[0] - tok)
+    allowed = keys_ok[None, :] & (later[None, :] <= slot[:, None])
+    bias = jnp.where(allowed, 0.0, -jnp.inf).astype(jnp.float32)
+    live = jnp.broadcast_to((half * tok + slot < live_len)[:, None], (tok, HD)).astype(jnp.float32)
+    span = keys_ok.shape[0]
+    kvw = prompt_keys.shape[2]
+    kv_here = kvw // HD
+    wr, wide = out_weight.shape
+    bf = jnp.bfloat16
+    dma = pltpu.SemaphoreType.DMA
+    vm = pl.BlockSpec(memory_space=pltpu.VMEM)
+    anywhere = pl.BlockSpec(memory_space=pl.ANY)
+    slots = 2 * CHUNKS
+    out = pl.pallas_call(
+        kernel,
+        out_shape=jax.ShapeDtypeStruct((tok, 2 * wide), bf),
+        in_specs=[vm, anywhere, anywhere, anywhere, anywhere, vm, vm, anywhere],
+        out_specs=vm,
+        scratch_shapes=[
+            pltpu.VMEM((span, kvw), bf),
+            pltpu.VMEM((span, kvw), bf),
+            pltpu.VMEM((kv_here, 2 * tok, wr), bf),
+            pltpu.VMEM((2, kv_here, wr, wide), bf),
+            pltpu.VMEM((2, 2 * tok, wide), bf),
+            pltpu.VMEM((2, 2, tok, wide), bf),
+            dma((2, 4)), dma((2, 4)), dma((2,)), dma((2,)), dma((4,)),
+            dma((2, kv_here, CHUNKS)), dma((4, CHUNKS)), dma((2, slots)), dma((2, slots)),
+            dma((kv_here,)), dma((kv_here,)), dma((2, 2)), dma((2, 2)),
+        ],
+        compiler_params=pltpu.CompilerParams(
+            collective_id=0, has_side_effects=True, vmem_limit_bytes=60 << 20
+        ),
+    )(
+        queries[0], prompt_keys[0], prompt_values[0], resp_keys[0], resp_values[0],
+        bias, live, out_weight,
+    )
+    return out[None]
+
+
 def solution(mesh):
     placed = (
         P("dp", "ctx", "tp"),
@@ -100,6 +450,8 @@
         P("dp", None),
         P(("tp", "dp"), "ctx"),
     )
+    sizes = (mesh.shape["ctx"], mesh.shape["tp"], mesh.shape["dp"])
+    body = fused if sizes == (4, 2, 4) else local
     return jax.shard_map(
-        local, mesh=mesh, in_specs=placed, out_specs=P("dp", "ctx", "tp"), check_vma=False
-    )
+        body, mesh=mesh, in_specs=placed, out_specs=P("dp", "ctx", "tp"), check_vma=False
+    )

time: 759 us -> 257 us (0.34)
  waiting for transfers between devices: 637 us -> 0 us
  Pallas kernels: 0 us -> 249 us
  matrix products: 64.9 us -> 0 us
  other arithmetic: 31.4 us -> 4.15 us
  between operations: 13.3 us -> 0.03 us
    all_gather x4 -> x0, waiting for transfers between devices: 591 us -> none  [the longest x1 517 us: local(): lax.all_gather(head_rows, 'ctx', axis=1, tiled=True)]
    pallas_call x0 -> x1, Pallas kernels: none -> 249 us  [fused(): pl.pallas_call(kernel, out_shape=jax.ShapeDtypeStruct((tok, 2 * wide), bf...]
    dot_general x5 -> x0, matrix products: 64.9 us -> none  [the longest x1 17.1 us: local(): jnp.einsum('kgij,jkd->kgid', weights.astype(jnp.bfloat16), piece_vals, pr...]
    reduce_scatter x1 -> x0, waiting for transfers between devices: 32 us -> none  [local(): lax.psum_scatter(partial_out.astype(jnp.bfloat16), 'tp', scatter_dimensio...]
    reduce_sum x5 -> x2, other arithmetic: 28.8 us -> 2.06 us  [the longest x1 1.29 us: fused(): live_len = jnp.sum(jnp.where(chosen, lengths[0], 0))]
    ppermute x2 -> x0, waiting for transfers between devices: 12.4 us -> none  [shifted(): return lax.ppermute(x, axis, pairs)]
  transfers between devices with their start and end apart: 7 -> 0, of which waited for: 7 -> 0; matrix products, arithmetic and copies ran while one was open for 12% -> 0% of each run, Pallas kernels for 0% -> 0%
where the time goes in v1:
time: 257 us; the launch traced here: 256 us
  Pallas kernels  249 us (97%)
  other arithmetic  4.15 us (2%)
  local copies, waits for them, and re-layouts  3.15 us (1%)
    pallas_call x1, Pallas kernels, fused(): pl.pallas_call(kernel, out_shape=jax.ShapeDtypeStruct((tok, 2 * wide), bf...  249 us

profile of v1, /device:TPU:17, one launch (start us, length us, event | category | flops | bytes accessed | tf_op | source)
XLA Modules:
  0.0 256.3 jit_solution(6914633715868496516)
XLA Ops:
  0.0 1.3 fusion.3
  1.3 0.6 compare_convert_fusion
  2.0 0.8 fusion.2
  2.7 0.1 broadcast_bitcast_fusion
  2.8 0.8 broadcast_in_dim.54.live_ref
  3.6 1.4 fusion.1.bias_ref
  5.0 249.0 %shard_map.82 = bf16[256,2048]{1,0:T(8,128)(2,1)} custom-call(bf16[256,4096]{1,0:T(8,128)(2,1)} %bitcast.17, bf16[256,512]{1,0:T(8,128)(2,1)} %bitcast.18, bf16[256,512]{1,0:T(8,128)(2,1)} %bitcast.19, bf16[256,512]{1,0:T(8,128)(2,1)} %bitcast.20, bf16[256,512]{1,0:T(8,128)(2,1)} %bitcast.21, f32[256,1536]{1,0:T(8,128)} %fusion.1.bias_ref, ...), custom_call_target="tpu_custom_call" | custom-call | tf_op jit(solution)/shard_map/pallas_call | solution.py:416
  254.0 2.3 copy.10
  (6 shorter events, 0.0 us)
